TPU v7x, 32 devices: a whole 2x2x4 slice. The times are simulated.
32 devices in a mesh: basis: 16 (over z, y, x), ex: 2 (over core).
Axes of the slice: x: 2, y: 2, z: 4, core: 2. Of those that a mesh axis runs over, the one named last changes fastest.
Arguments:
- activations: bfloat16 [64, 768, 2880], P(('basis', 'ex')), may hold values from -6 to 6
- out_grads: bfloat16 [64, 768, 2880], P(('basis', 'ex')), may hold values from -0.25 to 0.25
- grad_basis: bfloat16 [2880, 256], replicated, may hold values from -0.109375 to 0.109375
- panel_store: bfloat16 [16, 4, 2880, 128], P('basis', None, 'ex'), may hold values from -0.109375 to 0.109375
- owners: int32 [4], replicated, may hold values from 0 to 15, as said below
- token_count: int32 [64], P(('basis', 'ex')), may hold values from 96 to 768, as said below
Outputs:
- scaled: float32 [64, 256, 512], P('basis', 'ex')
Inputs may be any that keep to these rules, and one draw needn't show every extreme that they name: `owners`: values are basis indices; panels may share an owner. `token_count`: some example has all 768 tokens live.
All inputs are finite; a program needn't handle non-finite values.
Results may differ from a plain program's by a relative error of at most 0.00045.
The roundings to bfloat16 on the way count: a program that leaves them out, or rounds other values in their place, can miss the bound.
Values may be sent and summed in bfloat16 or wider, within the bound.
A program may use at most 128 MiB of HBM per device.

v0:
```python
import jax
import jax.numpy as jnp
from jax import lax
from jax.sharding import PartitionSpec as P


def broadcast(shard, axis, root):
    mine = lax.axis_index(axis) == root
    return lax.psum(jnp.where(mine, shard, jnp.zeros_like(shard)), axis)


def per_device(activations, out_grads, grad_basis, panel_store, owners, token_count):
    local_ex, tok_len, in_width = activations.shape
    act_rows = activations.reshape(local_ex * tok_len, in_width)
    own_slots = panel_store[0]
    n_panels = own_slots.shape[0]
    pieces = [
        broadcast(own_slots[panel_idx], "basis", owners[panel_idx]) for panel_idx in range(n_panels)
    ]
    panels = jnp.concatenate(pieces, axis=1)
    rotated = jnp.dot(
        act_rows,
        lax.all_gather(panels, "ex", axis=0, tiled=True),
        preferred_element_type=jnp.float32,
    )
    rotated = rotated.astype(jnp.bfloat16).reshape(local_ex, tok_len, -1)
    grads_rot = jnp.dot(
        out_grads.reshape(local_ex * tok_len, -1), grad_basis, preferred_element_type=jnp.float32
    )
    grads_rot = grads_rot.astype(jnp.bfloat16).reshape(local_ex, tok_len, -1)
    live_mask = jnp.arange(tok_len)[None, :] < token_count[:, None]
    grads_rot = jnp.where(live_mask[:, :, None], grads_rot, jnp.zeros((), jnp.bfloat16))
    ex_grads = lax.dot_general(
        grads_rot, rotated, (((1,), (1,)), ((0,), (0,))), preferred_element_type=jnp.float32
    )
    ex_count = local_ex * lax.axis_size("basis") * lax.axis_size("ex")
    entries = ex_grads.shape[1] * ex_grads.shape[2]
    sq_total = lax.psum(jnp.sum(ex_grads * ex_grads), ("basis", "ex"))
    eigen_rows = lax.all_to_all(ex_grads, "ex", split_axis=1, concat_axis=0, tiled=True)
    lambdas = lax.psum(jnp.sum(eigen_rows * eigen_rows, axis=0), "basis") / ex_count
    lam_mean = sq_total / ex_count / entries
    scaled = eigen_rows / (lambdas + 0.1 * lam_mean)
    return scaled


def solution(mesh):
    return jax.shard_map(
        per_device,
        mesh=mesh,
        in_specs=(
            P(("basis", "ex"), None, None),
            P(("basis", "ex"), None, None),
            P(),
            P("basis", None, "ex", None),
            P(),
            P(("basis", "ex")),
        ),
        out_specs=P("basis", "ex", None),
        check_vma=False,
    )
```

profile of v0, /device:TPU:0, one launch (start us, length us, event | category | flops | bytes accessed | tf_op | source)
XLA Modules:
  0.0 306.1 jit_solution(16652288639535279144)
XLA Ops:
  6.5 0.0 copy-start
  6.5 0.0 all-reduce.6.cloned.1.call-start
  6.5 1.5 fusion.6
  10.5 2.5 select_bitcast_fusion.3
  13.0 0.0 all-reduce.6.cloned.1.call-update
  13.0 0.0 all-gather.2.cloned.1.call-start
  13.1 119.9 %all-reduce.6.cloned.1.call-done = (bf16[1440,128]{1,0:T(8,128)(2,1)}, bf16[1440,128]{1,0:T(8,128)(2,1)}, bf16[1440,128]{1,0:T(8,128)(2,1)}, bf16[1440,128]{1,0:T(8,128)(2,1)}) async-done(((bf16[1440,128]{1,0:T(8,128)(2,1)}, bf16[1440,128]{1,0:T(8,128)(2,1)}, bf16[1440,128]{1,0:T(8,128)(2,1)}, bf16[1440,128]{1,0:T(8,128)(2,1)}), (bf16[1440,128]{1,0:T(8,128)(2,1)}, bf16[1440,128]{1,0:T(8,128)(2,1)}, ...) | async-done | bytes 1474576 | tf_op jit(solution)/shard_map/psum | solution.py:9
  133.0 2.6 pad_maximum_fusion
  135.6 0.0 all-gather.2.cloned.1.call-update
  135.7 0.0 all-reduce.4.cloned.1.call-start
  135.7 12.6 %copy.17 = bf16[2,768,2880]{2,1,0:T(8,128)(2,1)} copy(bf16[2,768,2880]{1,2,0:T(8,128)(2,1)} %param.6) | data formatting | bytes 17694720 | tf_op args[0]
  148.3 12.4 %copy.15 = bf16[2,768,2880]{2,1,0:T(8,128)(2,1)} copy(bf16[2,768,2880]{1,2,0:T(8,128)(2,1)} %param.7) | data formatting | bytes 17694720 | tf_op args[1]
  160.7 0.0 copy-done
  160.7 0.0 copy-start.1
  160.7 6.2 %convolution_convert_fusion.1 = bf16[1536,256]{1,0:T(8,128)(2,1)S(1)} fusion(bf16[1536,2880]{1,0:T(8,128)(2,1)} %bitcast.31, bf16[2880,256]{1,0:T(8,128)(2,1)S(1)} %copy-done), kind=kOutput, calls=%fused_computation.2 | convolution fusion | flops 2265317376 | bytes 11108352 | tf_op jit(solution)/shard_map/dot_general | solution.py:27
  166.9 1.2 copy.16
  168.1 0.0 copy-done.1
  168.1 0.1 iota_compare_fusion
  168.2 0.0 all-gather.2.cloned.1.call-done
  168.2 9.5 %fusion = bf16[1536,512]{0,1:T(8,128)(2,1)} fusion(bf16[2880,512]{1,0:T(8,128)(2,1)} %all-gather.2.cloned.1.call-done, bf16[1536,2880]{1,0:T(8,128)(2,1)} %bitcast.30), kind=kOutput, calls=%fused_computation.1 | convolution fusion | flops 4530634752 | bytes 13369344 | tf_op jit(solution)/shard_map/dot_general | solution.py:21
  177.7 1.7 copy.21
  179.4 2.4 multiply_reduce_fusion
  181.8 0.8 copy.19
  182.6 4.6 %all_to_all.18 = f32[2,256,512]{2,0,1:T(2,128)S(1)} all-to-all(f32[2,256,512]{2,0,1:T(2,128)S(1)} %copy.19), channel_id=1, replica_groups=mesh['basis'=16,'ex'=2] {'ex'}, dimensions={1} | all-to-all | bytes 2097152 | tf_op jit(solution)/shard_map/all_to_all | solution.py:39
  187.2 1.5 multiply_reduce_fusion.1
  188.7 0.0 all-reduce.4.cloned.1.call-update
  188.7 40.0 %psum.47 = f32[]{:T(128)} all-reduce(f32[]{:T(128)} %get-tuple-element.17), channel_id=1, replica_groups=mesh['basis'=16,'ex'=2] {'basis','ex'}, use_global_device_ids=true, to_apply=%region_7.8 | all-reduce | flops 1 | bytes 8 | tf_op jit(solution)/shard_map/psum | solution.py:38
  228.7 1.2 copy.20
  230.6 65.7 %all-reduce.4.cloned.1.call-done = f32[128,512]{1,0:T(8,128)} async-done(((f32[128,512]{1,0:T(8,128)}), f32[128,512]{1,0:T(8,128)}) %all-reduce.4.cloned.1.call-update) | async-done | bytes 262160 | tf_op jit(solution)/shard_map/psum | solution.py:40
  296.3 1.0 multiply_add_fusion
  297.2 2.3 bitcast_divide_fusion
Async XLA Ops:
  6.5 154.2 %copy-start = (bf16[2880,256]{1,0:T(8,128)(2,1)S(1)}, bf16[2880,256]{1,0:T(8,128)(2,1)}, u32[]{:S(2)}) copy-start(bf16[2880,256]{1,0:T(8,128)(2,1)} %param.8) | copy-start | bytes 4423684
  6.5 126.5 %all-reduce.6.cloned.1.call-start = ((), (), s32[]{:S(2)}) async-start(), calls=%async_computation.3 | async-start | bytes 2949120 | tf_op jit(solution)/shard_map/psum | solution.py:9
  13.0 155.2 %all-gather.2.cloned.1.call-start = ((), (), s32[]{:S(2)}) async-start(), calls=%async_computation.1 | async-start | bytes 4423680 | tf_op jit(solution)/shard_map/all_gather | solution.py:23
  135.7 160.6 %all-reduce.4.cloned.1.call-start = ((), (), s32[]{:S(2)}) async-start(), calls=%async_computation.2 | async-start | bytes 524288 | tf_op jit(solution)/shard_map/psum | solution.py:40
  160.7 7.4 %copy-start.1 = (s32[2]{0:T(128)S(1)}, s32[2]{0:T(128)}, u32[]{:S(2)}) copy-start(s32[2]{0:T(128)} %param.11) | copy-start | bytes 28
Sparse Core Ops, SparseCore 0:
  13.2 119.7 all-reduce.5
  135.8 11.3 all-gather.1
  188.9 107.3 all-reduce.3
where the time goes:
time: 307 us; the launch traced here: 306 us
  waiting for transfers between devices  186 us (61%)
  blocking collectives  44.5 us (14%)
  local copies, waits for them, and re-layouts  31.4 us (10%)
  matrix products  18.1 us (6%)
  between operations  16.3 us (5%)
  other arithmetic  9.98 us (3%)
    psum x1, waiting for transfers between devices, broadcast(): return lax.psum(jnp.where(mine, shard, jnp.zeros_like(shard)), axis)  120 us
    psum x1, waiting for transfers between devices, per_device(): lax.psum(jnp.sum(eigen_rows * eigen_rows, axis=0), 'basis') / ex_count  65.7 us
    psum x1, blocking collectives, per_device(): sq_total = lax.psum(jnp.sum(ex_grads * ex_grads), ('basis', 'ex'))  40 us
    unnamed x6, local copies, waits for them, and re-layouts  25 us
    dot_general x1, matrix products, per_device(): jnp.dot(act_rows, lax.all_gather(panels, 'ex', axis=0, tiled=True), prefe...  9.51 us
    dot_general x1, matrix products, per_device(): jnp.dot(out_grads.reshape(local_ex * tok_len, -1), grad_basis, preferred_...  6.2 us
  transfers between devices with their start and end apart: 3, of which 2 were waited for; matrix products, arithmetic and copies ran while one was open for 11% of the time, Pallas kernels for 0%

commit v1 on v0

v1 whole, which is shorter than its diff:
```python
import functools

import jax
import jax.numpy as jnp
from jax import lax
from jax.experimental import pallas as pl
from jax.experimental.pallas import tpu as pltpu
from jax.sharding import PartitionSpec as P

MESH = pl.DeviceIdType.MESH
LANE = 128
CHUNK = 256


def round_up(value, unit):
    return -(-value // unit) * unit


def split_kinds(rows, lanes, bits, row_unit):
    kinds = []
    for _ in range(bits):
        if (lanes // 2) % LANE == 0:
            kinds.append("lane")
            lanes //= 2
        elif (rows // 2) % row_unit == 0:
            kinds.append("row")
            rows //= 2
        else:
            return None
    return kinds


class Exchange:
    def __init__(self, base, rows, lanes, order, row_unit, basis, ex):
        self.order = order
        kinds = split_kinds(rows, lanes, len(order), row_unit)
        r0, l0 = 0, 0
        self.kept, self.sent, self.partner = [], [], []
        for kind, bit in zip(kinds, order):
            mine = (basis // (1 << bit)) % 2
            self.partner.append((basis + (1 - 2 * mine) * (1 << bit), ex))
            if kind == "lane":
                lanes //= 2
                self.kept.append((r0, rows, l0 + mine * lanes, lanes))
                self.sent.append((r0, rows, l0 + (1 - mine) * lanes, lanes))
            else:
                rows //= 2
                self.kept.append((r0 + mine * rows, rows, l0, lanes))
                self.sent.append((r0 + (1 - mine) * rows, rows, l0, lanes))
            r0, _, l0, _ = self.kept[-1]
        self.base = base
        self.row_unit = row_unit

    def at(self, region):
        r0, rows, l0, lanes = region
        row_start = self.base[0] + r0
        lane_start = self.base[1] + l0
        if not isinstance(row_start, int):
            row_start = pl.multiple_of(row_start, self.row_unit)
        if not isinstance(lane_start, int):
            lane_start = pl.multiple_of(lane_start, LANE)
        return pl.ds(row_start, rows), pl.ds(lane_start, lanes)


def stage_shapes(rows, lanes, bits, row_unit):
    shapes = []
    for kind in split_kinds(rows, lanes, bits, row_unit):
        if kind == "lane":
            lanes //= 2
        else:
            rows //= 2
        shapes.append((rows, lanes))
    return shapes


def kernel(
    cfg,
    owners_ref, count_ref, store_ref, gb_ref, act_ref, go_ref,
    out_ref,
    slots, gbv, gbt, act, go, work, full, acc, rot_g, rot_a, exg, exr, lam, lam_full, tot, tot_in,
    *rest,
):
    bits, n_ex, n_panels, half_rows, pad_rows, in_w, go_w, go_pad, tok, dirs, lam_parts = cfg
    recv = rest[:bits]
    lam_recv = rest[bits : 2 * bits]
    (store_sem, gb_sem, act_sem, go_sem, rs_s, rs_r, ag_s, ag_r, sb_s, sb_r,
     eg_s, eg_r, ls_s, ls_r, lg_s, lg_r, ts_s, ts_r) = rest[2 * bits :]
    basis = lax.axis_index("basis")
    ex = lax.axis_index("ex")
    sibling = (basis, 1 - ex)
    sends = []

    def remote(src, dst, s_sem, r_sem, to):
        copy = pltpu.make_async_remote_copy(
            src_ref=src, dst_ref=dst, send_sem=s_sem, recv_sem=r_sem, device_id=to, device_id_type=MESH
        )
        return copy

    def launch(copy):
        copy.start()
        sends.append(copy)
        return copy

    barrier = pltpu.get_barrier_semaphore()
    pl.semaphore_signal(barrier, inc=1, device_id=sibling, device_id_type=MESH)
    for bit in range(bits):
        mine = (basis // (1 << bit)) % 2
        peer = basis + (1 - 2 * mine) * (1 << bit)
        pl.semaphore_signal(barrier, inc=1, device_id=(peer, ex), device_id_type=MESH)

    half_panels = n_panels // 2
    issue = []
    for p in range(half_panels):
        issue += [p, p + half_panels]
    issue += [p for p in range(n_panels) if p not in issue]
    store_in = []
    for p in range(n_panels):
        store_in.append(pltpu.make_async_copy(
            store_ref.at[0, p], slots.at[p, pl.ds(0, half_rows)], store_sem.at[p]))
    for p in issue:
        store_in[p].start()
    gb_in = pltpu.make_async_copy(gb_ref, gbv.at[pl.ds(0, go_w)], gb_sem)
    gb_in.start()
    go_in = [pltpu.make_async_copy(go_ref.at[n], go.at[n, pl.ds(0, go_w)], go_sem.at[n]) for n in range(n_ex)]
    act_in = [pltpu.make_async_copy(act_ref.at[n], act.at[n, pl.ds(0, in_w)], act_sem.at[n]) for n in range(n_ex)]
    for copy in go_in + act_in:
        copy.start()

    first = list(range(bits))
    second = [1, 0] + first[2:] if bits > 1 else first
    parts = [
        Exchange((p * LANE, 0), LANE, pad_rows, first if p < half_panels else second, 16, basis, ex)
        for p in range(n_panels)
    ]

    if pad_rows > half_rows:
        for p in range(n_panels):
            slots[p, pl.ds(half_rows, pad_rows - half_rows), :] = jnp.zeros(
                (pad_rows - half_rows, LANE), slots.dtype)

    def rs_copy(p, j):
        return remote(work.at[parts[p].at(parts[p].sent[j])], recv[j].at[p],
                      rs_s.at[p, j], rs_r.at[p, j], parts[p].partner[j])

    rs = {}
    for i, p in enumerate(issue):
        store_in[p].wait()
        own = owners_ref[p] == basis
        for kb in range(pad_rows // LANE):
            block = slots[p, pl.ds(kb * LANE, LANE), :]
            block = jnp.where(own, block, jnp.zeros_like(block))
            work[pl.ds(p * LANE, LANE), pl.ds(kb * LANE, LANE)] = block.T
        if i == 0:
            pl.semaphore_wait(barrier, bits + 1)
        rs[p, 0] = launch(rs_copy(p, 0))

    gb_in.wait()
    if go_pad > go_w:
        gbv[pl.ds(go_w, go_pad - go_w), :] = jnp.zeros((go_pad - go_w, dirs), gbv.dtype)
        for n in range(n_ex):
            go[n, pl.ds(go_w, go_pad - go_w), :] = jnp.zeros((go_pad - go_w, tok), go.dtype)
    tail = act.shape[1] - in_w
    if tail > 0:
        for n in range(n_ex):
            act[n, pl.ds(in_w, tail), :] = jnp.zeros((tail, tok), act.dtype)
    for kb in range(go_pad // LANE):
        for db in range(dirs // LANE):
            gbt[pl.ds(db * LANE, LANE), pl.ds(kb * LANE, LANE)] = gbv[
                pl.ds(kb * LANE, LANE), pl.ds(db * LANE, LANE)].T

    go_ready = [False] * n_ex

    def rotate_grads(n, t):
        if not go_ready[n]:
            go_in[n].wait()
            go_ready[n] = True
        value = jnp.dot(gbt[...], go[n, :, pl.ds(t, CHUNK)], preferred_element_type=jnp.float32)
        value = value.astype(jnp.bfloat16)
        at = lax.broadcasted_iota(jnp.int32, value.shape, 1) + t
        rot_g[n, :, pl.ds(t, CHUNK)] = jnp.where(at < count_ref[n], value, jnp.zeros_like(value))

    jobs = [(n, t) for n in range(n_ex) for t in range(0, tok, CHUNK)]

    def some_jobs(number):
        for _ in range(min(number, len(jobs))):
            rotate_grads(*jobs.pop(0))

    def ag_copy(p, j):
        where = (ex,) + parts[p].at(parts[p].kept[j])
        return remote(full.at[where], full.at[where], ag_s.at[p, j], ag_r.at[p, j], parts[p].partner[j])

    def sb_copy(p, j):
        region = parts[p].kept[bits - 1] if j == bits else parts[p].sent[j]
        where = (ex,) + parts[p].at(region)
        return remote(full.at[where], full.at[where], sb_s.at[p, j], sb_r.at[p, j], sibling)

    def sb_wait(p, j):
        region = parts[p].kept[bits - 1] if j == bits else parts[p].sent[j]
        where = (1 - ex,) + parts[p].at(region)
        remote(full.at[where], full.at[where], sb_s.at[p, j], sb_r.at[p, j], sibling).wait_recv()

    ag = {}
    for j in range(bits):
        some_jobs(1)
        for p in issue:
            rs[p, j].wait_recv()
            kept = parts[p].at(parts[p].kept[j])
            total = work[kept] + recv[j][p]
            if j + 1 < bits:
                work[kept] = total
                rs[p, j + 1] = launch(rs_copy(p, j + 1))
            else:
                full[(ex,) + kept] = total
                ag[p, j] = launch(ag_copy(p, j))
                launch(sb_copy(p, bits))

    for j in range(bits - 1, 0, -1):
        some_jobs(1)
        for p in issue:
            ag[p, j].wait_recv()
            ag[p, j - 1] = launch(ag_copy(p, j - 1))
            launch(sb_copy(p, j))
    some_jobs(len(jobs))
    for copy in act_in:
        copy.wait()

    half_k = pad_rows // 2
    pair_rows = half_panels * LANE

    def rotate_acts(pair, other, side, stage):
        bit = parts[pair * half_panels].order[0]
        mine = (basis // (1 << bit)) % 2
        pick = 1 - mine if other else mine
        k_at = pl.multiple_of(pick * half_k, LANE)
        row_at = pl.multiple_of(side * half_rows + pick * half_k, 16)
        rows = pl.ds(pair * pair_rows, pair_rows)
        lhs = full[side, rows, pl.ds(k_at, half_k)]
        for n in range(n_ex):
            for t in range(0, tok, CHUNK):
                value = jnp.dot(lhs, act[n, pl.ds(row_at, half_k), pl.ds(t, CHUNK)],
                                preferred_element_type=jnp.float32)
                cols = pl.ds(t, CHUNK)
                if stage > 0:
                    value = value + acc[n, rows, cols]
                if stage == 2:
                    rot_a[n, rows, cols] = value.astype(jnp.bfloat16)
                else:
                    acc[n, rows, cols] = value

    members = [issue_p for issue_p in ([p for p in issue if p < half_panels],
                                       [p for p in issue if p >= half_panels])]
    for pair in range(2):
        rotate_acts(pair, False, ex, 0)
    for pair in range(2):
        for p in members[pair]:
            for j in range(bits, 0, -1):
                sb_wait(p, j)
        rotate_acts(pair, False, 1 - ex, 1)
    for p in issue:
        ag[p, 0].wait_recv()
        launch(sb_copy(p, 0))
    for pair in range(2):
        rotate_acts(pair, True, ex, 1)
    for pair in range(2):
        for p in members[pair]:
            sb_wait(p, 0)
        rotate_acts(pair, True, 1 - ex, 2)

    share = dirs // 2
    theirs = pl.ds(pl.multiple_of((1 - ex) * share, 8), share)
    ours = pl.ds(pl.multiple_of(ex * share, 8), share)
    eg = []
    tile_sum = jnp.zeros((8, LANE), jnp.float32)
    for n in range(n_ex):
        value = lax.dot_general(rot_g[n], rot_a[n], (((1,), (1,)), ((), ())),
                                preferred_element_type=jnp.float32)
        exg[n] = value
        eg.append(launch(remote(exg.at[n, theirs], exr.at[n], eg_s.at[n], eg_r.at[n], sibling)))
        squares = value * value
        columns = squares[:, :LANE]
        for c in range(LANE, squares.shape[1], LANE):
            columns = columns + squares[:, c : c + LANE]
        tile_sum = tile_sum + jnp.sum(columns.reshape(dirs // 8, 8, LANE), axis=0)
    tot[0] = tile_sum

    def tot_copy(j):
        if j == 0:
            to = sibling
        else:
            to = lam_ex[0].partner[j - 1]
        return remote(tot.at[j], tot_in.at[j], ts_s.at[j], ts_r.at[j], to)

    width = lam.shape[1]
    lam_lanes = width // lam_parts
    lam_ex = [
        Exchange((0, c * lam_lanes), share, lam_lanes, first if c == 0 else second, 8, basis, ex)
        for c in range(lam_parts)
    ]
    tots = [launch(tot_copy(0))]
    for copy in eg:
        copy.wait_recv()
    partial = jnp.zeros((share, width), jnp.float32)
    for n in range(n_ex):
        here, there = exg[n, ours, :], exr[n]
        partial = partial + (here * here + there * there)
    lam[...] = partial

    def ls_copy(c, j):
        return remote(lam.at[lam_ex[c].at(lam_ex[c].sent[j])], lam_recv[j].at[c],
                      ls_s.at[c, j], ls_r.at[c, j], lam_ex[c].partner[j])

    def lg_copy(c, j):
        where = lam_ex[c].at(lam_ex[c].kept[j])
        return remote(lam_full.at[where], lam_full.at[where], lg_s.at[c, j], lg_r.at[c, j],
                      lam_ex[c].partner[j])

    def next_total(j):
        tots[j].wait_recv()
        tot[j + 1] = tot[j] + tot_in[j]

    ls, lg = {}, {}
    for c in range(lam_parts):
        ls[c, 0] = launch(ls_copy(c, 0))
    next_total(0)
    tots.append(launch(tot_copy(1)))
    for j in range(bits):
        for c in range(lam_parts):
            ls[c, j].wait_recv()
            kept = lam_ex[c].at(lam_ex[c].kept[j])
            total = lam[kept] + lam_recv[j][c]
            if j + 1 < bits:
                lam[kept] = total
                ls[c, j + 1] = launch(ls_copy(c, j + 1))
            else:
                lam_full[kept] = total
                lg[c, j] = launch(lg_copy(c, j))
        next_total(j + 1)
        if j + 1 < bits:
            tots.append(launch(tot_copy(j + 2)))
    for j in range(bits - 1, 0, -1):
        for c in range(lam_parts):
            lg[c, j].wait_recv()
            lg[c, j - 1] = launch(lg_copy(c, j - 1))
    ex_count = n_ex * 2 * (1 << bits)
    damp = 0.1 * (jnp.sum(tot[bits + 1], keepdims=True) / ex_count / (dirs * width))
    for c in range(lam_parts):
        lg[c, 0].wait_recv()
    scale = lam_full[...] / ex_count + damp
    for n in range(n_ex):
        out_ref[ex * n_ex + n] = exg[n, ours, :] / scale
        out_ref[(1 - ex) * n_ex + n] = exr[n] / scale
    for copy in sends:
        copy.wait_send()


def per_device(activations, out_grads, grad_basis, panel_store, owners, token_count):
    n_ex, tok, in_w = activations.shape
    go_w = out_grads.shape[2]
    dirs = grad_basis.shape[1]
    _, n_panels, half_rows, panel = panel_store.shape
    n_basis = lax.axis_size("basis")
    bits = n_basis.bit_length() - 1
    assert 1 << bits == n_basis and lax.axis_size("ex") == 2
    pad_rows = round_up(half_rows, 2 * LANE)
    while split_kinds(panel, pad_rows, bits, 16) is None:
        pad_rows += 2 * LANE
    go_pad = round_up(go_w, LANE)
    act_rows = max(in_w, half_rows + pad_rows)
    width = n_panels * panel
    share = dirs // 2
    lam_parts = 2 if split_kinds(share, width // 2, bits, 8) else 1
    cfg = (bits, n_ex, n_panels, half_rows, pad_rows, in_w, go_w, go_pad, tok, dirs, lam_parts)
    bf16, f32 = jnp.bfloat16, jnp.float32
    dma = pltpu.SemaphoreType.DMA
    scratch = [
        pltpu.VMEM((n_panels, pad_rows, panel), bf16),
        pltpu.VMEM((go_pad, dirs), bf16),
        pltpu.VMEM((dirs, go_pad), bf16),
        pltpu.VMEM((n_ex, act_rows, tok), bf16),
        pltpu.VMEM((n_ex, go_pad, tok), bf16),
        pltpu.VMEM((width, pad_rows), bf16),
        pltpu.VMEM((2, width, pad_rows), bf16),
        pltpu.VMEM((n_ex, width, tok), f32),
        pltpu.VMEM((n_ex, dirs, tok), bf16),
        pltpu.VMEM((n_ex, width, tok), bf16),
        pltpu.VMEM((n_ex, dirs, width), f32),
        pltpu.VMEM((n_ex, share, width), f32),
        pltpu.VMEM((share, width), f32),
        pltpu.VMEM((share, width), f32),
        pltpu.VMEM((bits + 2, 8, LANE), f32),
        pltpu.VMEM((bits + 1, 8, LANE), f32),
    ]
    for rows, lanes in stage_shapes(panel, pad_rows, bits, 16):
        scratch.append(pltpu.VMEM((n_panels, rows, lanes), bf16))
    for rows, lanes in stage_shapes(share, width // lam_parts, bits, 8):
        scratch.append(pltpu.VMEM((lam_parts, rows, lanes), f32))
    scratch += [dma((n_panels,)), dma, dma((n_ex,)), dma((n_ex,))]
    scratch += [dma((n_panels, bits))] * 4 + [dma((n_panels, bits + 1))] * 2
    scratch += [dma((n_ex,))] * 2 + [dma((lam_parts, bits))] * 4 + [dma((bits + 1,))] * 2
    smem = pl.BlockSpec(memory_space=pltpu.SMEM)
    anywhere = pl.BlockSpec(memory_space=pl.ANY)
    return pl.pallas_call(
        functools.partial(kernel, cfg),
        out_shape=jax.ShapeDtypeStruct((2 * n_ex, share, width), f32),
        in_specs=[smem, smem, anywhere, anywhere, anywhere, anywhere],
        out_specs=pl.BlockSpec(memory_space=pltpu.VMEM),
        scratch_shapes=scratch,
        compiler_params=pltpu.CompilerParams(
            collective_id=0, has_side_effects=True, vmem_limit_bytes=60 * 1024 * 1024),
        name="ekfac",
    )(owners, token_count, panel_store, grad_basis,
      jnp.swapaxes(activations, 1, 2), jnp.swapaxes(out_grads, 1, 2))


def solution(mesh):
    return jax.shard_map(
        per_device,
        mesh=mesh,
        in_specs=(
            P(("basis", "ex"), None, None),
            P(("basis", "ex"), None, None),
            P(),
            P("basis", None, "ex", None),
            P(),
            P(("basis", "ex")),
        ),
        out_specs=P("basis", "ex", None),
        check_vma=False,
    )
```

time: 307 us -> 82.5 us (0.27)
  waiting for transfers between devices: 186 us -> 0 us
  Pallas kernels: 0 us -> 80.1 us
  blocking collectives: 44.5 us -> 0 us
  local copies, waits for them, and re-layouts: 31.4 us -> 2.26 us
  matrix products: 18.1 us -> 0 us
  between operations: 16.3 us -> 0.01 us
  other arithmetic: 9.98 us -> 0 us
    psum x2 -> x0, waiting for transfers between devices: 186 us -> none  [the longest x1 120 us: broadcast(): return lax.psum(jnp.where(mine, shard, jnp.zeros_like(shard)), axis)]
    pallas_call x0 -> x1, Pallas kernels: none -> 80.1 us  [per_device(): pl.pallas_call(functools.partial(kernel, cfg), out_shape=jax.ShapeDtypeSt...]
    psum x1 -> x0, blocking collectives: 40 us -> none  [per_device(): sq_total = lax.psum(jnp.sum(ex_grads * ex_grads), ('basis', 'ex'))]
    unnamed x6 -> x1, local copies, waits for them, and re-layouts: 25 us -> 2.26 us
    dot_general x3 -> x0, matrix products: 18.1 us -> none  [the longest x1 9.51 us: per_device(): jnp.dot(act_rows, lax.all_gather(panels, 'ex', axis=0, tiled=True), prefe...]
    all_to_all x1 -> x0, blocking collectives: 4.58 us -> none  [per_device(): lax.all_to_all(ex_grads, 'ex', split_axis=1, concat_axis=0, tiled=True)]
  transfers between devices with their start and end apart: 3 -> 0, of which waited for: 2 -> 0; matrix products, arithmetic and copies ran while one was open for 11% -> 0% of each run, Pallas kernels for 0% -> 0%
where the time goes in v1:
time: 82.5 us; the launch traced here: 82.4 us
  Pallas kernels  80.1 us (97%)
  local copies, waits for them, and re-layouts  2.26 us (3%)
    pallas_call x1, Pallas kernels, per_device(): pl.pallas_call(functools.partial(kernel, cfg), out_shape=jax.ShapeDtypeSt...  80.1 us
    unnamed x1, local copies, waits for them, and re-layouts  2.26 us

profile of v1, /device:TPU:0, one launch (start us, length us, event | category | flops | bytes accessed | tf_op | source)
XLA Modules:
  0.0 82.4 jit_solution(16504225796859231984)
XLA Ops:
  0.0 80.1 %ekfac.1 = f32[4,128,512]{2,1,0:T(8,128)} custom-call(s32[4]{0:T(128)} %owners_ref.1, s32[2]{0:T(128)} %count_ref.1, bf16[1,4,1440,128]{3,2,1,0:T(8,128)(2,1)} %store_ref.1, bf16[2880,256]{1,0:T(8,128)(2,1)} %gb_ref.1, bf16[2,2880,768]{2,1,0:T(8,128)(2,1)} %bitcast.2, bf16[2,2880,768]{2,1,0:T(8,128)(2,1)} %bitcast.3), custom_call_target="tpu_custom_call" | custom-call | tf_op jit(solution)/shard_map/ekfac/pallas_call | solution.py:402
  80.1 2.3 %copy.8 = f32[4,128,512]{2,1,0:T(8,128)} copy(f32[4,128,512]{2,1,0:T(8,128)} %ekfac.1) | data formatting | bytes 2097152

commit v2 on v0

v2 whole, which is shorter than its diff:
```python
import functools

import jax
import jax.numpy as jnp
from jax import lax
from jax.experimental import pallas as pl
from jax.experimental.pallas import tpu as pltpu
from jax.sharding import PartitionSpec as P

MESH = pl.DeviceIdType.MESH
LANE = 128
CHUNK = 256


def round_up(value, unit):
    return -(-value // unit) * unit


class Quarter:
    def __init__(self, base, rows, lanes, order, basis, ex):
        self.kept, self.sent, self.partner = [], [], []
        at = 0
        for bit in order:
            mine = (basis // (1 << bit)) % 2
            lanes //= 2
            self.partner.append((basis + (1 - 2 * mine) * (1 << bit), ex))
            self.kept.append((base, rows, at + mine * lanes, lanes))
            self.sent.append((base, rows, at + (1 - mine) * lanes, lanes))
            at = at + mine * lanes


def window(region):
    base, rows, at, lanes = region
    return pl.ds(base, rows), pl.ds(pl.multiple_of(at, LANE), lanes)


def kernel(
    cfg,
    owners_ref, count_ref, store_ref, gb_ref, act_ref, go_ref,
    out_ref,
    slots, gbv, gbt, act, go, work, full, acc, rot_g, rot_a, exg, exr,
    in0, in1, own, up_in, up_out, down_in, down_out,
    lam, lam_in1, lam_mid, lam_in2, lam_full, tot, tot_sib, tot_in1, tot_in2,
    store_sem, gb_sem, act_sem, go_sem, rs_s, rs_r, ag_s, ag_r, sb_s, sb_r,
    up_s, up_r, dn_s, dn_r, eg_s, eg_r, l1_s, l1_r, l2_s, l2_r, l3_s, l3_r,
    t0_s, t0_r, t1_s, t1_r, t2_s, t2_r,
):
    n_basis, n_ex, n_panels, half_rows, pad_rows, in_w, go_w, go_pad, tok, dirs = cfg
    basis = lax.axis_index("basis")
    ex = lax.axis_index("ex")
    sibling = (basis, 1 - ex)
    levels = n_basis // 4
    quad = basis % 4
    level = basis // 4
    sends = []

    def quad_at(m):
        low, high = quad % 2, quad // 2
        low = 1 - low if m % 2 else low
        high = 1 - high if m // 2 else high
        return low + 2 * high

    quad_peers = {m: (level * 4 + quad_at(m), ex) for m in (1, 2, 3)}
    level_peers = {s: (((level + s) % levels) * 4 + quad, ex) for s in range(1, levels)}

    def remote(src, dst, s_sem, r_sem, to):
        return pltpu.make_async_remote_copy(
            src_ref=src, dst_ref=dst, send_sem=s_sem, recv_sem=r_sem, device_id=to, device_id_type=MESH
        )

    def launch(copy):
        copy.start()
        sends.append(copy)
        return copy

    barrier = pltpu.get_barrier_semaphore()
    greeted = [sibling] + list(quad_peers.values()) + list(level_peers.values())
    for peer in greeted:
        pl.semaphore_signal(barrier, inc=1, device_id=peer, device_id_type=MESH)

    groups = [[p, p + 1] for p in range(0, n_panels, 2)]
    store_in = []
    for p in range(n_panels):
        store_in.append(pltpu.make_async_copy(
            store_ref.at[0, p], slots.at[p, pl.ds(0, half_rows)], store_sem.at[p]))
        store_in[p].start()
    gb_in = pltpu.make_async_copy(gb_ref, gbv.at[pl.ds(0, go_w)], gb_sem)
    gb_in.start()
    go_in = [pltpu.make_async_copy(go_ref.at[n], go.at[n, pl.ds(0, go_w)], go_sem.at[n]) for n in range(n_ex)]
    act_in = [pltpu.make_async_copy(act_ref.at[n], act.at[n, pl.ds(0, in_w)], act_sem.at[n]) for n in range(n_ex)]
    for copy in go_in + act_in:
        copy.start()

    parts = [
        Quarter(p * LANE, LANE, pad_rows, (1, 0) if p % 2 else (0, 1), basis, ex) for p in range(n_panels)
    ]
    halves_in = (in0, in1)

    if pad_rows > half_rows:
        for p in range(n_panels):
            slots[p, pl.ds(half_rows, pad_rows - half_rows), :] = jnp.zeros(
                (pad_rows - half_rows, LANE), slots.dtype)

    def rs_copy(p, j):
        return remote(work.at[window(parts[p].sent[j])], halves_in[j].at[p],
                      rs_s.at[p, j], rs_r.at[p, j], parts[p].partner[j])

    def prepare(p):
        store_in[p].wait()
        mine = owners_ref[p] == basis
        for kb in range(pad_rows // LANE):
            block = slots[p, pl.ds(kb * LANE, LANE), :]
            block = jnp.where(mine, block, jnp.zeros_like(block))
            work[pl.ds(p * LANE, LANE), pl.ds(kb * LANE, LANE)] = block.T

    rs = {}

    def start_halving(group):
        for p in group:
            rs[p, 0] = launch(rs_copy(p, 0))

    def second_halving(group):
        for p in group:
            rs[p, 0].wait_recv()
            at = window(parts[p].kept[0])
            work[at] = work[at] + in0[p]
            rs[p, 1] = launch(rs_copy(p, 1))

    def up_copy(src, p):
        return remote(src.at[p], up_in.at[p], up_s.at[p], up_r.at[p], (basis + 4, ex))

    def down_copy(src, p):
        return remote(src.at[p], down_in.at[p], dn_s.at[p], dn_r.at[p], (basis - 4, ex))

    def start_scan(group):
        for p in group:
            rs[p, 1].wait_recv()
            at = window(parts[p].kept[1])
            value = work[at] + in1[p]
            own[p] = value
            full[(ex,) + at] = value

        if levels > 1:
            @pl.when(level == 0)
            def _():
                for p in group:
                    up_copy(own, p).start()

            @pl.when(level == levels - 1)
            def _():
                for p in group:
                    down_copy(own, p).start()

    def scan_round(group, r):
        def step(copy, arrived, onward, forward):
            for p in group:
                at = window(parts[p].kept[1])
                copy(own, p).wait_recv()
                if forward:
                    onward[p] = own[p] + arrived[p]
                    copy(onward, p).start()
                full[(ex,) + at] = full[(ex,) + at] + arrived[p]

        @pl.when(level == r + 1)
        def _():
            step(up_copy, up_in, up_out, r + 1 < levels - 1)

        @pl.when(level == levels - 2 - r)
        def _():
            step(down_copy, down_in, down_out, r + 1 < levels - 1)

    def finish_scan_sends():
        if levels == 1:
            return

        @pl.when(level < levels - 1)
        def _():
            for p in range(n_panels):
                up_copy(own, p).wait_send()

        @pl.when(level > 0)
        def _():
            for p in range(n_panels):
                down_copy(own, p).wait_send()

    def ag_copy(p, j):
        where = (ex,) + window(parts[p].kept[j])
        return remote(full.at[where], full.at[where], ag_s.at[p, j], ag_r.at[p, j], parts[p].partner[j])

    def sb_copy(p, j, side):
        region = parts[p].kept[1] if j == 2 else parts[p].sent[j]
        where = (side,) + window(region)
        return remote(full.at[where], full.at[where], sb_s.at[p, j], sb_r.at[p, j], sibling)

    ag = {}

    def start_gather(group):
        for p in group:
            ag[p, 1] = launch(ag_copy(p, 1))
        for p in group:
            launch(sb_copy(p, 2, ex))

    def second_gather(group):
        for p in group:
            ag[p, 1].wait_recv()
            ag[p, 0] = launch(ag_copy(p, 0))
        for p in group:
            launch(sb_copy(p, 1, ex))

    def end_gather(group):
        for p in group:
            ag[p, 0].wait_recv()
            launch(sb_copy(p, 0, ex))

    def await_sibling(group):
        for j in (2, 1, 0):
            for p in group:
                sb_copy(p, j, 1 - ex).wait_recv()

    go_ready = [False] * n_ex

    def rotate_grads(n, t):
        if not go_ready[n]:
            go_in[n].wait()
            go_ready[n] = True
        value = jnp.dot(gbt[...], go[n, :, pl.ds(t, CHUNK)], preferred_element_type=jnp.float32)
        value = value.astype(jnp.bfloat16)
        at = lax.broadcasted_iota(jnp.int32, value.shape, 1) + t
        rot_g[n, :, pl.ds(t, CHUNK)] = jnp.where(at < count_ref[n], value, jnp.zeros_like(value))

    jobs = [(n, t) for n in range(n_ex) for t in range(0, tok, CHUNK)]

    def some_jobs(number):
        for _ in range(min(number, len(jobs))):
            rotate_grads(*jobs.pop(0))

    group_w = 2 * LANE

    def rotate_acts(g, side, last):
        rows = pl.ds(g * group_w, group_w)
        row_at = pl.multiple_of(side * half_rows, 16)
        for n in range(n_ex):
            for t in range(0, tok, CHUNK):
                cols = pl.ds(t, CHUNK)
                value = jnp.dot(full[side, rows, :], act[n, pl.ds(row_at, pad_rows), cols],
                                preferred_element_type=jnp.float32)
                if last:
                    rot_a[n, rows, cols] = (value + acc[n, :, cols]).astype(jnp.bfloat16)
                else:
                    acc[n, :, cols] = value

    share = dirs // 2
    part_rows = share // 4
    theirs = pl.ds(pl.multiple_of((1 - ex) * share, 8), share)
    ours = pl.ds(pl.multiple_of(ex * share, 8), share)
    eg = {}
    tile_sums = []

    def gradients(g):
        cols = pl.ds(g * group_w, group_w)
        for n in range(n_ex):
            value = lax.dot_general(rot_g[n], rot_a[n, cols, :], (((1,), (1,)), ((), ())),
                                    preferred_element_type=jnp.float32)
            exg[n, :, cols] = value
            eg[g, n] = launch(remote(exg.at[n, theirs, cols], exr.at[n, :, cols],
                                     eg_s.at[g, n], eg_r.at[g, n], sibling))
            squares = value * value
            columns = squares[:, :LANE] + squares[:, LANE:]
            tile_sums.append(jnp.sum(columns.reshape(dirs // 8, 8, LANE), axis=0))

    l1, l2, l3 = {}, {}, {}

    def quad_rows(index):
        return pl.ds(pl.multiple_of(index * part_rows, 8), part_rows)

    def lam_one(g):
        cols = pl.ds(g * group_w, group_w)
        partial = jnp.zeros((share, group_w), jnp.float32)
        for n in range(n_ex):
            eg[g, n].wait_recv()
            here, there = exg[n, ours, cols], exr[n, :, cols]
            partial = partial + (here * here + there * there)
        lam[g] = partial
        for m in (3, 1, 2):
            l1[g, m] = launch(remote(lam.at[g, quad_rows(quad_at(m))], lam_in1.at[g, m - 1],
                                     l1_s.at[g, m - 1], l1_r.at[g, m - 1], quad_peers[m]))

    def lam_two(g):
        total = lam[g, quad_rows(quad), :]
        for m in (1, 2, 3):
            l1[g, m].wait_recv()
            total = total + lam_in1[g, m - 1]
        lam_mid[g] = total
        for s in range(1, levels):
            l2[g, s] = launch(remote(lam_mid.at[g], lam_in2.at[g, s - 1],
                                     l2_s.at[g, s - 1], l2_r.at[g, s - 1], level_peers[s]))

    def lam_three(g):
        total = lam_mid[g]
        for s in range(1, levels):
            l2[g, s].wait_recv()
            total = total + lam_in2[g, s - 1]
        at = quad_rows(quad)
        lam_full[g, at, :] = total
        for m in (3, 1, 2):
            l3[g, m] = launch(remote(lam_full.at[g, at], lam_full.at[g, at],
                                     l3_s.at[g, m - 1], l3_r.at[g, m - 1], quad_peers[m]))

    def lam_end(g):
        for m in (1, 2, 3):
            l3[g, m].wait_recv()

    first, second = groups
    last_round = levels - 2
    for p in first:
        prepare(p)
    pl.semaphore_wait(barrier, len(greeted))
    start_halving(first)
    for p in second:
        prepare(p)
    gb_in.wait()
    if go_pad > go_w:
        gbv[pl.ds(go_w, go_pad - go_w), :] = jnp.zeros((go_pad - go_w, dirs), gbv.dtype)
        for n in range(n_ex):
            go[n, pl.ds(go_w, go_pad - go_w), :] = jnp.zeros((go_pad - go_w, tok), go.dtype)
    tail = act.shape[1] - in_w
    if tail > 0:
        for n in range(n_ex):
            act[n, pl.ds(in_w, tail), :] = jnp.zeros((tail, tok), act.dtype)
    for kb in range(go_pad // LANE):
        for db in range(dirs // LANE):
            gbt[pl.ds(db * LANE, LANE), pl.ds(kb * LANE, LANE)] = gbv[
                pl.ds(kb * LANE, LANE), pl.ds(db * LANE, LANE)].T
    second_halving(first)
    start_halving(second)
    some_jobs(2)
    start_scan(first)
    some_jobs(1)
    for r in range(levels - 1):
        scan_round(first, r)
        if r == 0:
            second_halving(second)
            some_jobs(1)
    start_gather(first)
    start_scan(second)
    some_jobs(1)
    for r in range(levels - 1):
        scan_round(second, r)
        if r == 0:
            second_gather(first)
            some_jobs(len(jobs))
    if levels == 1:
        second_halving(second)
        second_gather(first)
    start_gather(second)
    some_jobs(len(jobs))
    for copy in act_in:
        copy.wait()
    end_gather(first)
    second_gather(second)
    rotate_acts(0, ex, False)
    await_sibling(first)
    rotate_acts(0, 1 - ex, True)
    gradients(0)
    lam_one(0)
    end_gather(second)
    rotate_acts(1, ex, False)
    lam_two(0)
    await_sibling(second)
    rotate_acts(1, 1 - ex, True)
    gradients(1)
    lam_three(0)

    whole = tile_sums[0]
    for tile in tile_sums[1:]:
        whole = whole + tile
    tot[0] = whole
    t0 = launch(remote(tot.at[0], tot_sib, t0_s, t0_r, sibling))
    lam_one(1)
    t0.wait_recv()
    tot[1] = tot[0] + tot_sib[...]
    t1 = {m: launch(remote(tot.at[1], tot_in1.at[m - 1], t1_s.at[m - 1], t1_r.at[m - 1], quad_peers[m]))
          for m in (1, 2, 3)}
    lam_two(1)
    whole = tot[1]
    for m in (1, 2, 3):
        t1[m].wait_recv()
        whole = whole + tot_in1[m - 1]
    tot[2] = whole
    t2 = {s: launch(remote(tot.at[2], tot_in2.at[s - 1], t2_s.at[s - 1], t2_r.at[s - 1], level_peers[s]))
          for s in range(1, levels)}
    lam_three(1)
    whole = tot[2]
    for s in range(1, levels):
        t2[s].wait_recv()
        whole = whole + tot_in2[s - 1]
    ex_count = n_ex * 2 * n_basis
    width = n_panels * LANE
    damp = 0.1 * (jnp.sum(whole, keepdims=True) / ex_count / (dirs * width))
    for g in range(2):
        lam_end(g)
        cols = pl.ds(g * group_w, group_w)
        scale = lam_full[g] / ex_count + damp
        for n in range(n_ex):
            out_ref[ex * n_ex + n, :, cols] = exg[n, ours, cols] / scale
            out_ref[(1 - ex) * n_ex + n, :, cols] = exr[n, :, cols] / scale
    for copy in sends:
        copy.wait_send()
    finish_scan_sends()


def per_device(activations, out_grads, grad_basis, panel_store, owners, token_count):
    n_ex, tok, in_w = activations.shape
    go_w = out_grads.shape[2]
    dirs = grad_basis.shape[1]
    _, n_panels, half_rows, panel = panel_store.shape
    n_basis = lax.axis_size("basis")
    assert n_basis % 4 == 0 and lax.axis_size("ex") == 2 and n_panels == 4 and panel == LANE
    pad_rows = round_up(half_rows, 4 * LANE)
    go_pad = round_up(go_w, LANE)
    act_rows = max(in_w, half_rows + pad_rows)
    width = n_panels * panel
    share = dirs // 2
    levels = n_basis // 4
    others = max(levels - 1, 1)
    group_w = 2 * panel
    cfg = (n_basis, n_ex, n_panels, half_rows, pad_rows, in_w, go_w, go_pad, tok, dirs)
    bf16, f32 = jnp.bfloat16, jnp.float32
    dma = pltpu.SemaphoreType.DMA
    quarter = pltpu.VMEM((n_panels, panel, pad_rows // 4), bf16)
    scratch = [
        pltpu.VMEM((n_panels, pad_rows, panel), bf16),
        pltpu.VMEM((go_pad, dirs), bf16),
        pltpu.VMEM((dirs, go_pad), bf16),
        pltpu.VMEM((n_ex, act_rows, tok), bf16),
        pltpu.VMEM((n_ex, go_pad, tok), bf16),
        pltpu.VMEM((width, pad_rows), bf16),
        pltpu.VMEM((2, width, pad_rows), bf16),
        pltpu.VMEM((n_ex, group_w, tok), f32),
        pltpu.VMEM((n_ex, dirs, tok), bf16),
        pltpu.VMEM((n_ex, width, tok), bf16),
        pltpu.VMEM((n_ex, dirs, width), f32),
        pltpu.VMEM((n_ex, share, width), f32),
        pltpu.VMEM((n_panels, panel, pad_rows // 2), bf16),
        quarter, quarter, quarter, quarter, quarter, quarter,
        pltpu.VMEM((2, share, group_w), f32),
        pltpu.VMEM((2, 3, share // 4, group_w), f32),
        pltpu.VMEM((2, share // 4, group_w), f32),
        pltpu.VMEM((2, others, share // 4, group_w), f32),
        pltpu.VMEM((2, share, group_w), f32),
        pltpu.VMEM((3, 8, LANE), f32),
        pltpu.VMEM((8, LANE), f32),
        pltpu.VMEM((3, 8, LANE), f32),
        pltpu.VMEM((others, 8, LANE), f32),
    ]
    scratch += [dma((n_panels,)), dma, dma((n_ex,)), dma((n_ex,))]
    scratch += [dma((n_panels, 2))] * 4 + [dma((n_panels, 3))] * 2 + [dma((n_panels,))] * 4
    scratch += [dma((2, n_ex))] * 2 + [dma((2, 3))] * 2 + [dma((2, others))] * 2 + [dma((2, 3))] * 2
    scratch += [dma] * 2 + [dma((3,))] * 2 + [dma((others,))] * 2
    smem = pl.BlockSpec(memory_space=pltpu.SMEM)
    anywhere = pl.BlockSpec(memory_space=pl.ANY)
    return pl.pallas_call(
        functools.partial(kernel, cfg),
        out_shape=jax.ShapeDtypeStruct((2 * n_ex, share, width), f32),
        in_specs=[smem, smem, anywhere, anywhere, anywhere, anywhere],
        out_specs=pl.BlockSpec(memory_space=pltpu.VMEM),
        scratch_shapes=scratch,
        compiler_params=pltpu.CompilerParams(
            collective_id=0, has_side_effects=True, vmem_limit_bytes=60 * 1024 * 1024),
        name="ekfac",
    )(owners, token_count, panel_store, grad_basis,
      jnp.swapaxes(activations, 1, 2), jnp.swapaxes(out_grads, 1, 2))


def solution(mesh):
    return jax.shard_map(
        per_device,
        mesh=mesh,
        in_specs=(
            P(("basis", "ex"), None, None),
            P(("basis", "ex"), None, None),
            P(),
            P("basis", None, "ex", None),
            P(),
            P(("basis", "ex")),
        ),
        out_specs=P("basis", "ex", None),
        check_vma=False,
    )
```

time: 307 us -> 73.6 us (0.24)
  waiting for transfers between devices: 186 us -> 0 us
  Pallas kernels: 0 us -> 71.2 us
  blocking collectives: 44.5 us -> 0 us
  local copies, waits for them, and re-layouts: 31.4 us -> 2.26 us
  matrix products: 18.1 us -> 0 us
  between operations: 16.3 us -> 0.01 us
  other arithmetic: 9.98 us -> 0 us
    psum x2 -> x0, waiting for transfers between devices: 186 us -> none  [the longest x1 120 us: broadcast(): return lax.psum(jnp.where(mine, shard, jnp.zeros_like(shard)), axis)]
    pallas_call x0 -> x1, Pallas kernels: none -> 71.2 us  [per_device(): pl.pallas_call(functools.partial(kernel, cfg), out_shape=jax.ShapeDtypeSt...]
    psum x1 -> x0, blocking collectives: 40 us -> none  [per_device(): sq_total = lax.psum(jnp.sum(ex_grads * ex_grads), ('basis', 'ex'))]
    unnamed x6 -> x1, local copies, waits for them, and re-layouts: 25 us -> 2.26 us
    dot_general x3 -> x0, matrix products: 18.1 us -> none  [the longest x1 9.51 us: per_device(): jnp.dot(act_rows, lax.all_gather(panels, 'ex', axis=0, tiled=True), prefe...]
    all_to_all x1 -> x0, blocking collectives: 4.58 us -> none  [per_device(): lax.all_to_all(ex_grads, 'ex', split_axis=1, concat_axis=0, tiled=True)]
  transfers between devices with their start and end apart: 3 -> 0, of which waited for: 2 -> 0; matrix products, arithmetic and copies ran while one was open for 11% -> 0% of each run, Pallas kernels for 0% -> 0%
where the time goes in v2:
time: 73.6 us; the launch traced here: 73.5 us
  Pallas kernels  71.2 us (97%)
  local copies, waits for them, and re-layouts  2.26 us (3%)
    pallas_call x1, Pallas kernels, per_device(): pl.pallas_call(functools.partial(kernel, cfg), out_shape=jax.ShapeDtypeSt...  71.2 us
    unnamed x1, local copies, waits for them, and re-layouts  2.26 us

profile of v2, /device:TPU:0, one launch (start us, length us, event | category | flops | bytes accessed | tf_op | source)
XLA Modules:
  0.0 73.5 jit_solution(2367368741452937306)
XLA Ops:
  0.0 71.2 %ekfac.1 = f32[4,128,512]{2,1,0:T(8,128)} custom-call(s32[4]{0:T(128)} %owners_ref.1, s32[2]{0:T(128)} %count_ref.1, bf16[1,4,1440,128]{3,2,1,0:T(8,128)(2,1)} %store_ref.1, bf16[2880,256]{1,0:T(8,128)(2,1)} %gb_ref.1, bf16[2,2880,768]{2,1,0:T(8,128)(2,1)} %bitcast.2, bf16[2,2880,768]{2,1,0:T(8,128)(2,1)} %bitcast.3), custom_call_target="tpu_custom_call" | custom-call | tf_op jit(solution)/shard_map/ekfac/pallas_call | solution.py:462
  71.2 2.3 %copy.8 = f32[4,128,512]{2,1,0:T(8,128)} copy(f32[4,128,512]{2,1,0:T(8,128)} %ekfac.1) | data formatting | bytes 2097152
